TPU v7x, 128 devices: a whole 4x4x4 slice. The times are simulated.
128 devices in a mesh: row: 16 (over y, x), col: 8 (over z, core).
Axes of the slice: x: 4, y: 4, z: 4, core: 2. Of those that a mesh axis runs over, the one named last changes fastest.
Arguments:
- spectra: bfloat16 [16384, 4096], P(('row', 'col')), may hold values from 0 to 16, as said below
- projection: bfloat16 [4096, 1024], replicated, may hold values from -0.09375 to 0.09375
- kernel_slot: int32 [16384], P(('row', 'col')), may hold values from 0 to 16383, as said below
- env_image: int32 [16384], P(('row', 'col')), may hold values from 0 to 1023, never falling along the last dimension, each value on 1 to 48 neighbouring positions
- image_atoms: int32 [1024], replicated, may hold values from 8 to 64
Outputs:
- panels: float32 [16384, 1024], P('row')
- trailing: float32 [16384, 16384], P('row', 'col')
Inputs may be any that keep to these rules, and one draw needn't show every extreme that they name: `spectra`: Nonnegative. A permutation. With the block of environment e being kernel_slot[e] // 128: among the 128 environments of one device (aligned blocks of 128 in environment order) at most 1 fall in any one block, and in every draw some block receives 1 of them.
All inputs are finite; a program needn't handle non-finite values.
Results may differ from a plain program's by a relative error of at most 0.0063.
Values may be sent and summed in bfloat16 or wider, within the bound.
No kernel may reach another device: no remote copies, remote signals or barrier semaphores. Data moves between devices by JAX's collectives and lax.ppermute only.
A program may use at most 128 MiB of HBM per device.

v0:
```python
import jax
import jax.numpy as jnp
from jax import lax
from jax.sharding import PartitionSpec as P

NB = 512
PANELS = 2
ATOM_RIDGE = 0.02
NORM_EPS = 1e-06


def from_root(block, axis, source):
    block = jnp.where(lax.axis_index(axis) == source, block, jnp.zeros_like(block))
    return lax.psum(block, axis)


def same_block(blocks):
    return blocks


def outgoing(unit_rows, kernel_slot, block_owner, per_device, capacity, devices):
    target = block_owner(kernel_slot // per_device)
    positions = jnp.arange(per_device, dtype=jnp.int32)
    earlier = (target[:, None] == target[None, :]) & (positions[None, :] < positions[:, None])
    rank_within = jnp.sum(earlier.astype(jnp.int32), axis=1)
    source_rows = (
        jnp.zeros((devices * capacity,), jnp.int32)
        .at[target * capacity + rank_within]
        .set(positions)
    )
    return jnp.take(unit_rows, source_rows, axis=0)


def incoming(received, slot_all, own_index, block_owner, per_device, capacity, devices):
    slot_table = slot_all.reshape(devices, per_device)
    arrives_here = block_owner(slot_table // per_device) == own_index
    rank_within = jnp.cumsum(arrives_here.astype(jnp.int32), axis=1) - 1
    sources = jnp.arange(devices, dtype=jnp.int32)[:, None]
    buffer_rows = sources * capacity + rank_within
    landing = jnp.where(arrives_here, slot_table % per_device, per_device)
    pick_rows = (
        jnp.zeros((per_device,), jnp.int32)
        .at[landing.reshape(-1)]
        .set(buffer_rows.reshape(-1), mode="drop")
    )
    return jnp.take(received, pick_rows, axis=0)


def body(spectra, projection, kernel_slot, env_image, image_atoms):
    grid_rows = lax.axis_size("row")
    grid_cols = lax.axis_size("col")
    devices = grid_rows * grid_cols
    per_device = spectra.shape[0]
    total_rows = per_device * devices
    reduced_width = projection.shape[1]
    row_group = total_rows // grid_rows
    col_group = total_rows // grid_cols
    capacity = max(1, per_device // devices)
    row_index = lax.axis_index("row")
    col_index = lax.axis_index("col")
    own_index = row_index * grid_cols + col_index
    projected = jnp.dot(spectra, projection, preferred_element_type=jnp.float32)
    factor = lax.rsqrt(
        jnp.mean(projected * projected, axis=1, keepdims=True) + NORM_EPS
    ) * reduced_width ** (-0.5)
    unit_rows = (projected * factor).astype(jnp.bfloat16)
    slot_all, image_all = (
        lax.all_gather(kernel_slot, ("row", "col"), axis=0, tiled=True),
        lax.all_gather(env_image, ("row", "col"), axis=0, tiled=True),
    )
    sent_rows = outgoing(unit_rows, kernel_slot, same_block, per_device, capacity, devices)
    received_rows = lax.all_to_all(
        sent_rows, ("row", "col"), split_axis=0, concat_axis=0, tiled=True
    )
    own_rows = incoming(
        received_rows, slot_all, own_index, same_block, per_device, capacity, devices
    )
    row_group_rows = lax.all_gather(own_rows, "col", axis=0, tiled=True)
    group_list = []
    for copy_index in range(grid_rows // grid_cols):
        group_list.append(from_root(row_group_rows, "row", col_index + copy_index * grid_cols))
    col_group_rows = jnp.concatenate(group_list, axis=0)
    gram_matrix = lax.dot_general(
        row_group_rows, col_group_rows, (((1,), (1,)), ((), ())), preferred_element_type=jnp.float32
    )
    inverse = (
        jnp.zeros((total_rows,), jnp.int32)
        .at[slot_all]
        .set(jnp.arange(total_rows, dtype=jnp.int32))
    )
    env_rows = lax.dynamic_slice_in_dim(inverse, row_index * row_group, row_group)
    image_rows = jnp.take(image_all, env_rows)
    image_count = image_atoms.shape[0]
    atom_count = jnp.sum(
        jnp.where(
            image_rows[:, None] == jnp.arange(image_count, dtype=jnp.int32)[None, :],
            image_atoms[None, :],
            0,
        ),
        axis=1,
    )
    ridge_diag = ATOM_RIDGE * atom_count.astype(jnp.float32)
    offset = row_index // grid_cols * row_group
    holds_diagonal = col_index == row_index % grid_cols
    row_positions = jnp.arange(row_group, dtype=jnp.int32)
    col_positions = jnp.arange(col_group, dtype=jnp.int32)
    diagonal_hit = (col_positions[None, :] == offset + row_positions[:, None]) & holds_diagonal
    covariance = gram_matrix * gram_matrix + jnp.where(diagonal_hit, ridge_diag[:, None], 0.0)
    row_tile = row_positions // NB * grid_rows + row_index
    panel_list = []
    for panel_index in range(PANELS):
        root_row = panel_index % grid_rows
        root_col = panel_index % grid_cols
        row_start = panel_index // grid_rows * NB
        col_start = root_row // grid_cols * row_group + row_start
        corner = lax.slice(covariance, (row_start, col_start), (row_start + NB, col_start + NB))
        pivot_tile = from_root(corner, "row", root_row)
        lower_factor = jnp.linalg.cholesky(pivot_tile)
        column = lax.slice_in_dim(covariance, col_start, col_start + NB, axis=1)
        solved = lax.linalg.triangular_solve(
            lower_factor, column, left_side=False, lower=True, transpose_a=True
        )
        solved = jnp.where((row_tile >= panel_index)[:, None], solved, 0.0)
        panel_row = from_root(solved, "col", root_col)
        copies = []
        for copy_index in range(grid_rows // grid_cols):
            copies.append(from_root(panel_row, "row", col_index + copy_index * grid_cols))
        panel_cols = jnp.concatenate(copies, axis=0)
        update = lax.dot_general(
            panel_row,
            panel_cols,
            (((1,), (1,)), ((), ())),
            precision=lax.Precision.HIGHEST,
            preferred_element_type=jnp.float32,
        )
        covariance = covariance - update
        panel_list.append(panel_row)
    panels = jnp.concatenate(panel_list, axis=1)
    return (panels, covariance)


def solution(mesh):
    in_specs = (P(("row", "col"), None), P(), P(("row", "col")), P(("row", "col")), P())
    out_specs = (P("row", None), P("row", "col"))
    return jax.shard_map(body, mesh=mesh, in_specs=in_specs, out_specs=out_specs, check_vma=False)
```

profile of v0, /device:TPU:1, one launch (start us, length us, event | category | flops | bytes accessed | tf_op | source)
XLA Modules:
  0.0 1150.8 jit_solution(3452723511936852365)
XLA Ops:
  7.9 34.4 %all-gather = s32[128,1,128]{2,1,0:T(1,128)S(1)} all-gather(s32[1,1,128]{2,1,0:T(1,128)} %bitcast.141), channel_id=1, replica_groups=mesh['row'=16,'col'=8] {'row','col'}, dimensions={0}, use_global_device_ids=true | all-gather | bytes 66048 | tf_op jit(solution)/shard_map/all_gather | solution.py:68
  44.7 60.3 %scatter_custom_fusion.1 = s32[128]{0:T(128)S(1)} fusion(s32[16384]{0:T(1024)S(1)} %get-tuple-element.84, s32[16384]{0:T(1024)S(1)} %bitcast.140, s32[]{:T(128)} %copy.130), kind=kCustom, calls=%fused_computation.223 | custom fusion | bytes 516 | tf_op jit(solution)/shard_map/scatter | solution.py:44
  132.8 22.2 %all-gather.4.cloned.1.call-done = bf16[1024,1024]{1,0:T(8,128)(2,1)} async-done(((bf16[128,1024]{1,0:T(8,128)(2,1)}), bf16[1024,1024]{1,0:T(8,128)(2,1)}) %all-gather.4.cloned.1.call-update) | async-done | bytes 2097168 | tf_op jit(solution)/shard_map/all_gather | solution.py:78
  159.0 60.3 %scatter_custom_fusion.2 = s32[16384]{0:T(1024)S(1)} fusion(s32[16384]{0:T(1024)S(1)} %get-tuple-element.83, s32[16384]{0:T(1024)S(1)} %iota.95, s32[]{:T(128)} %copy.130), kind=kCustom, calls=%fused_computation.176 | custom fusion | bytes 65540 | tf_op jit(solution)/shard_map/scatter | solution.py:89
  219.4 31.0 %all-gather.1 = s32[128,1,128]{2,1,0:T(1,128)S(1)} all-gather(s32[1,1,128]{2,1,0:T(1,128)S(1)} %bitcast.142), channel_id=1, replica_groups=mesh['row'=16,'col'=8] {'row','col'}, dimensions={0}, use_global_device_ids=true | all-gather | bytes 66048 | tf_op jit(solution)/shard_map/all_gather | solution.py:69
  274.3 85.6 %all-reduce.12.cloned.1.call-done = f32[512,512]{0,1:T(8,128)} async-done(((f32[512,512]{0,1:T(8,128)}), f32[512,512]{0,1:T(8,128)}) %all-reduce.12.cloned.1.call-update) | async-done | bytes 1048592 | tf_op jit(solution)/shard_map/psum | solution.py:14
  361.9 11.7 %cholesky.286 = f32[128,128]{1,0:T(8,128)S(1)} custom-call(f32[128,128]{1,0:T(8,128)S(1)} %cholesky.426), custom_call_target="Cholesky" | custom-call | tf_op jit(solution)/shard_map/jit(cholesky)/cholesky | solution.py:118
  384.2 11.7 %cholesky.305 = f32[128,128]{1,0:T(8,128)S(1)} custom-call(f32[128,128]{1,0:T(8,128)S(1)} %cholesky.430), custom_call_target="Cholesky" | custom-call | tf_op jit(solution)/shard_map/jit(cholesky)/cholesky | solution.py:118
  408.0 11.7 %cholesky.326 = f32[128,128]{1,0:T(8,128)S(1)} custom-call(f32[128,128]{1,0:T(8,128)S(1)} %cholesky.435), custom_call_target="Cholesky" | custom-call | tf_op jit(solution)/shard_map/jit(cholesky)/cholesky | solution.py:118
  430.8 11.7 %cholesky.343 = f32[128,128]{1,0:T(8,128)S(1)} custom-call(f32[128,128]{1,0:T(8,128)S(1)} %convolution_subtract_fusion.9), custom_call_target="Cholesky" | custom-call | tf_op jit(solution)/shard_map/jit(cholesky)/cholesky | solution.py:118
  454.8 39.3 %custom-call.30 = f32[4,128,128]{1,2,0:T(8,128)S(1)} custom-call(f32[4,128,128]{2,1,0:T(8,128)S(1)} %get-tuple-element.19), custom_call_target="InvertDiagBlocksLowerTriangular" | custom-call | tf_op jit(solution)/shard_map/triangular_solve/custom-call.3 | solution.py:120
  505.0 64.9 %all-reduce.14.cloned.1.call-done = f32[1024,512]{0,1:T(8,128)} async-done(((f32[1024,512]{0,1:T(8,128)}), f32[1024,512]{0,1:T(8,128)}) %all-reduce.14.cloned.1.call-update) | async-done | bytes 2097168 | tf_op jit(solution)/shard_map/psum | solution.py:14
  574.4 104.4 %all-reduce.22.cloned.1.call-done = (f32[1024,512]{0,1:T(8,128)}, f32[1024,512]{0,1:T(8,128)}) async-done(((f32[1024,512]{0,1:T(8,128)}, f32[1024,512]{0,1:T(8,128)}), (f32[1024,512]{0,1:T(8,128)}, f32[1024,512]{0,1:T(8,128)})) %all-reduce.22.cloned.1.call-update) | async-done | bytes 4194320 | tf_op jit(solution)/shard_map/psum | solution.py:14
  678.8 16.4 %fusion.15 = f32[1024,2048]{0,1:T(8,128)S(1)} fusion(f32[1024,2048]{0,1:T(8,128)} %copy-done.3, f32[1024,512]{0,1:T(8,128)S(1)} %copy-done.4, f32[1024,512]{0,1:T(8,128)} %get-tuple-element.49, f32[1024,512]{0,1:T(8,128)} %get-tuple-element.50), kind=kOutput, calls=%fused_computation.28 | convolution fusion | flops 12888047616 | bytes 23068672 | tf_op jit(solution)/shard_map/dot_general | solution.py:129
  700.0 85.6 %all-reduce.16.cloned.1.call-done = f32[512,512]{0,1:T(8,128)} async-done(((f32[512,512]{0,1:T(8,128)}), f32[512,512]{0,1:T(8,128)}) %all-reduce.16.cloned.1.call-update) | async-done | bytes 1048592 | tf_op jit(solution)/shard_map/psum | solution.py:14
  790.7 11.7 %cholesky.358 = f32[128,128]{1,0:T(8,128)S(1)} custom-call(f32[128,128]{1,0:T(8,128)S(1)} %cholesky.439), custom_call_target="Cholesky" | custom-call | tf_op jit(solution)/shard_map/jit(cholesky)/cholesky | solution.py:118
  814.9 11.7 %cholesky.377 = f32[128,128]{1,0:T(8,128)S(1)} custom-call(f32[128,128]{1,0:T(8,128)S(1)} %cholesky.443), custom_call_target="Cholesky" | custom-call | tf_op jit(solution)/shard_map/jit(cholesky)/cholesky | solution.py:118
  839.6 11.7 %cholesky.398 = f32[128,128]{1,0:T(8,128)S(1)} custom-call(f32[128,128]{1,0:T(8,128)S(1)} %cholesky.448), custom_call_target="Cholesky" | custom-call | tf_op jit(solution)/shard_map/jit(cholesky)/cholesky | solution.py:118
  863.3 11.7 %cholesky.415 = f32[128,128]{1,0:T(8,128)S(1)} custom-call(f32[128,128]{1,0:T(8,128)S(1)} %convolution_subtract_fusion.8), custom_call_target="Cholesky" | custom-call | tf_op jit(solution)/shard_map/jit(cholesky)/cholesky | solution.py:118
  879.7 11.7 %while.5 = (s32[]{:T(128)}, f32[512,512]{1,0:T(8,128)}, s32[4,2]{0,1:T(2,128)S(1)}, f32[4,128,128]{2,1,0:T(8,128)S(1)}, s32[]{:T(128)}) while((s32[]{:T(128)}, f32[512,512]{1,0:T(8,128)}, s32[4,2]{0,1:T(2,128)S(1)}, f32[4,128,128]{2,1,0:T(8,128)S(1)}, s32[]{:T(128)}) %tuple.91), condition=%wide.while_cond.clone, body=%wide.while_body.clone.sunk | while | flops 2 | bytes 131181 | solution.py:120
  891.4 39.3 %custom-call.34 = f32[4,128,128]{1,2,0:T(8,128)S(1)} custom-call(f32[4,128,128]{2,1,0:T(8,128)S(1)} %get-tuple-element.20), custom_call_target="InvertDiagBlocksLowerTriangular" | custom-call | tf_op jit(solution)/shard_map/triangular_solve/custom-call.3 | solution.py:120
  942.1 64.8 %all-reduce.18.cloned.1.call-done = f32[1024,512]{0,1:T(8,128)} async-done(((f32[1024,512]{0,1:T(8,128)}), f32[1024,512]{0,1:T(8,128)}) %all-reduce.18.cloned.1.call-update) | async-done | bytes 2097168 | tf_op jit(solution)/shard_map/psum | solution.py:14
  1020.8 94.9 %all-reduce.20.cloned.1.call-done = (f32[1024,512]{0,1:T(8,128)}, f32[1024,512]{0,1:T(8,128)}) async-done(((f32[1024,512]{0,1:T(8,128)}, f32[1024,512]{0,1:T(8,128)}), (f32[1024,512]{0,1:T(8,128)}, f32[1024,512]{0,1:T(8,128)})) %all-reduce.20.cloned.1.call-update) | async-done | bytes 4194320 | tf_op jit(solution)/shard_map/psum | solution.py:14
  1115.8 18.8 %fusion.12 = f32[1024,2048]{0,1:T(8,128)} fusion(f32[1024,2048]{0,1:T(8,128)} %copy-done.2, f32[1024,512]{0,1:T(8,128)S(1)} %copy-done.5, f32[1024,512]{0,1:T(8,128)} %get-tuple-element.47, f32[1024,512]{0,1:T(8,128)} %get-tuple-element.48), kind=kOutput, calls=%fused_computation.27 | convolution fusion | flops 12888047616 | bytes 23068672 | tf_op jit(solution)/shard_map/dot_general | solution.py:129
  (182 shorter events, 222.7 us)
Async XLA Ops:
  7.2 97.9 %copy-start = (bf16[128,4096]{1,0:T(8,128)(2,1)S(1)}, bf16[128,4096]{1,0:T(8,128)(2,1)}, u32[]{:S(2)}) copy-start(bf16[128,4096]{1,0:T(8,128)(2,1)} %param.10) | copy-start | bytes 3145732
  113.1 17.7 %all-to-all-start = ((bf16[128,2,512]{2,1,0:T(2,128)(2,1)}), bf16[128,2,512]{2,1,0:T(2,128)(2,1)S(1)}, u32[]{:S(2)}, u32[]{:S(2)}) async-start(bf16[128,2,512]{2,1,0:T(2,128)(2,1)} %reshape.208), calls=%async_computation | async-start | bytes 524288 | tf_op jit(solution)/shard_map/all_to_all | solution.py:72
  119.8 35.2 %all-gather.4.cloned.1.call-start = ((), (), s32[]{:S(2)}) async-start(), calls=%async_computation.1 | async-start | bytes 2359296 | tf_op jit(solution)/shard_map/all_gather | solution.py:78
  132.7 129.2 %all-reduce.24.cloned.1.call-start = ((), (), s32[]{:S(2)}) async-start(), calls=%async_computation.8 | async-start | bytes 8388608 | tf_op jit(solution)/shard_map/psum | solution.py:14
  158.9 60.5 %copy-start.11 = (s32[128]{0:T(128)S(1)}, s32[128]{0:T(128)}, u32[]{:S(2)}) copy-start(s32[128]{0:T(128)} %param.13) | copy-start | bytes 1540
  158.9 201.0 %all-reduce.12.cloned.1.call-start = ((), (), s32[]{:S(2)}) async-start(), calls=%async_computation.2 | async-start | bytes 2097152 | tf_op jit(solution)/shard_map/psum | solution.py:14
  250.4 6.2 copy-start.10
  250.4 11.5 copy-start.9
  269.6 3.4 copy-start.3
  274.1 295.9 %all-reduce.14.cloned.1.call-start = ((), (), s32[]{:S(2)}) async-start(), calls=%async_computation.3 | async-start | bytes 4194304 | tf_op jit(solution)/shard_map/psum | solution.py:14
  359.9 1.7 copy-start.6
  505.0 173.8 %all-reduce.22.cloned.1.call-start = ((), (), s32[]{:S(2)}) async-start(), calls=%async_computation.7 | async-start | bytes 8388608 | tf_op jit(solution)/shard_map/psum | solution.py:14
  574.3 104.5 %copy-start.4 = (f32[1024,512]{0,1:T(8,128)S(1)}, f32[1024,512]{0,1:T(8,128)}, u32[]{:S(2)}) copy-start(f32[1024,512]{0,1:T(8,128)} %all-reduce.14.cloned.1.call-done) | copy-start | bytes 6291460
  574.3 211.4 %all-reduce.16.cloned.1.call-start = ((), (), s32[]{:S(2)}) async-start(), calls=%async_computation.4 | async-start | bytes 2097152 | tf_op jit(solution)/shard_map/psum | solution.py:14
  695.3 3.4 copy-start.2
  699.8 307.1 %all-reduce.18.cloned.1.call-start = ((), (), s32[]{:S(2)}) async-start(), calls=%async_computation.5 | async-start | bytes 4194304 | tf_op jit(solution)/shard_map/psum | solution.py:14
  785.7 2.6 copy-start.7
  789.7 1.0 copy-start.8
  941.9 173.9 %all-reduce.20.cloned.1.call-start = ((), (), s32[]{:S(2)}) async-start(), calls=%async_computation.6 | async-start | bytes 8388608 | tf_op jit(solution)/shard_map/psum | solution.py:14
  1015.3 100.4 %copy-start.5 = (f32[1024,512]{0,1:T(8,128)S(1)}, f32[1024,512]{0,1:T(8,128)}, u32[]{:S(2)}) copy-start(f32[1024,512]{0,1:T(8,128)} %all-reduce.18.cloned.1.call-done) | copy-start | bytes 6291460
  1134.5 9.2 copy-start.1
Sparse Core Ops, SparseCore 0:
  132.8 22.1 all-gather.3
  159.0 102.8 all-reduce.23
  274.2 85.7 all-reduce.11
  505.1 64.8 all-reduce.13
  574.4 104.3 all-reduce.21
  699.9 85.7 all-reduce.15
  942.0 64.8 all-reduce.17
  1011.4 104.3 all-reduce.19
where the time goes:
time: 1160 us; the launch traced here: 1150 us
  waiting for transfers between devices  538 us (46%)
  other arithmetic  268 us (23%)
  local copies, waits for them, and re-layouts  178 us (15%)
  matrix products  73.4 us (6%)
  blocking collectives  65.4 us (6%)
  between operations  20.2 us (2%)
    psum x7, waiting for transfers between devices, from_root(): return lax.psum(block, axis)  505 us
    another operation x30, other arithmetic, body(): lower_factor = jnp.linalg.cholesky(pivot_tile)  158 us
    another operation x5, other arithmetic, body(): lax.linalg.triangular_solve(lower_factor, column, left_side=False, lower=...  80.6 us
    scatter x1, local copies, waits for them, and re-layouts, body(): inverse = jnp.zeros((total_rows,), jnp.int32).at[slot_all].set(jnp.arange...  60.3 us
    scatter x1, local copies, waits for them, and re-layouts, incoming(): pick_rows = jnp.zeros((per_device,), jnp.int32).at[landing.reshape(-1)].s...  60.3 us
    dot_general x2, matrix products, body(): lax.dot_general(panel_row, panel_cols, (((1,), (1,)), ((), ())), precisio...  35.2 us
    all_gather x1, blocking collectives, body(): lax.all_gather(kernel_slot, ('row', 'col'), axis=0, tiled=True)  34.4 us
    all_gather x1, blocking collectives, body(): lax.all_gather(env_image, ('row', 'col'), axis=0, tiled=True)  31 us
  transfers between devices with their start and end apart: 9, of which 9 were waited for; matrix products, arithmetic and copies ran while one was open for 7% of the time, Pallas kernels for 0%

commit v1 on v0

--- a/solution.py
+++ b/solution.py
@@ -11,7 +11,7 @@
 
 def from_root(block, axis, source):
     block = jnp.where(lax.axis_index(axis) == source, block, jnp.zeros_like(block))
-    return lax.psum(block, axis)
+    return jnp.sum(lax.all_gather(block, axis), axis=0)
 
 
 def same_block(blocks):

time: 1160 us -> 2280 us (1.97)
  waiting for transfers between devices: 538 us -> 1410 us
  local copies, waits for them, and re-layouts: 178 us -> 337 us
  other arithmetic: 268 us -> 353 us
    all_gather x0 -> x10, waiting for transfers between devices: none -> 1370 us  [from_root(): return jnp.sum(lax.all_gather(block, axis), axis=0)]
    psum x7 -> x0, waiting for transfers between devices: 505 us -> none  [from_root(): return lax.psum(block, axis)]
    unnamed x29 -> x30, local copies, waits for them, and re-layouts: 23.7 us -> 185 us
    reduce_sum x0 -> x10, other arithmetic: none -> 88.8 us  [from_root(): return jnp.sum(lax.all_gather(block, axis), axis=0)]
  transfers between devices with their start and end apart: 9 -> 12, of which waited for: 9 -> 12; matrix products, arithmetic and copies ran while one was open for 7% -> 8% of each run, Pallas kernels for 0% -> 0%
where the time goes in v1:
time: 2280 us; the launch traced here: 2270 us
  waiting for transfers between devices  1410 us (62%)
  other arithmetic  353 us (15%)
  local copies, waits for them, and re-layouts  337 us (15%)
  matrix products  78.7 us (3%)
  blocking collectives  66.8 us (3%)
    all_gather x10, waiting for transfers between devices, from_root(): return jnp.sum(lax.all_gather(block, axis), axis=0)  1370 us
    unnamed x30, local copies, waits for them, and re-layouts  185 us
    another operation x30, other arithmetic, body(): lower_factor = jnp.linalg.cholesky(pivot_tile)  159 us
    reduce_sum x10, other arithmetic, from_root(): return jnp.sum(lax.all_gather(block, axis), axis=0)  88.8 us
    another operation x5, other arithmetic, body(): lax.linalg.triangular_solve(lower_factor, column, left_side=False, lower=...  79.9 us
    scatter x1, local copies, waits for them, and re-layouts, body(): inverse = jnp.zeros((total_rows,), jnp.int32).at[slot_all].set(jnp.arange...  60.3 us
    scatter x1, local copies, waits for them, and re-layouts, incoming(): pick_rows = jnp.zeros((per_device,), jnp.int32).at[landing.reshape(-1)].s...  60.3 us
  transfers between devices with their start and end apart: 12, of which 12 were waited for; matrix products, arithmetic and copies ran while one was open for 8% of the time, Pallas kernels for 0%

profile of v1, /device:TPU:1, one launch (start us, length us, event | category | flops | bytes accessed | tf_op | source)
XLA Modules:
  0.0 2271.7 jit_solution(14226465767199208994)
XLA Ops:
  7.9 34.4 %all-gather.10 = s32[128,1,128]{2,1,0:T(1,128)S(1)} all-gather(s32[1,1,128]{2,1,0:T(1,128)} %bitcast.185), channel_id=1, replica_groups=mesh['row'=16,'col'=8] {'row','col'}, dimensions={0}, use_global_device_ids=true | all-gather | bytes 66048 | tf_op jit(solution)/shard_map/all_gather | solution.py:68
  44.7 60.3 %scatter_custom_fusion.1 = s32[128]{0:T(128)S(1)} fusion(s32[16384]{0:T(1024)S(1)} %get-tuple-element.78, s32[16384]{0:T(1024)S(1)} %bitcast.184, s32[]{:T(128)} %copy.76), kind=kCustom, calls=%fused_computation.229 | custom fusion | bytes 516 | tf_op jit(solution)/shard_map/scatter | solution.py:44
  132.8 22.2 all-gather.24.cloned.1.call-done
  159.7 60.3 %scatter_custom_fusion.2 = s32[16384]{0:T(1024)S(1)} fusion(s32[16384]{0:T(1024)S(1)} %get-tuple-element.77, s32[16384]{0:T(1024)S(1)} %iota.95, s32[]{:T(128)} %copy.76), kind=kCustom, calls=%fused_computation.182 | custom fusion | bytes 65540 | tf_op jit(solution)/shard_map/scatter | solution.py:89
  220.1 32.4 %all-gather.11 = s32[128,1,128]{2,1,0:T(1,128)S(1)} all-gather(s32[1,1,128]{2,1,0:T(1,128)S(1)} %bitcast.186), channel_id=1, replica_groups=mesh['row'=16,'col'=8] {'row','col'}, dimensions={0}, use_global_device_ids=true | all-gather | bytes 66048 | tf_op jit(solution)/shard_map/all_gather | solution.py:69
  259.5 96.1 %all-gather.26.cloned.1.call-done = bf16[16384,1024]{1,0:T(8,128)(2,1)} async-done(((bf16[1024,1024]{1,0:T(8,128)(2,1)}), bf16[16384,1024]{1,0:T(8,128)(2,1)}) %all-gather.26.cloned.1.call-update) | async-done | bytes 33554448 | tf_op jit(solution)/shard_map/all_gather | solution.py:14
  367.4 187.5 %all-gather.28.cloned.1.call-done = bf16[16384,1024]{1,0:T(8,128)(2,1)} async-done(((bf16[1024,1024]{1,0:T(8,128)(2,1)}), bf16[16384,1024]{1,0:T(8,128)(2,1)}) %all-gather.28.cloned.1.call-update) | async-done | bytes 33554448 | tf_op jit(solution)/shard_map/all_gather | solution.py:14
  580.3 110.7 %all-gather.30.cloned.1.call-done = f32[8192,512]{1,0:T(8,128)} async-done(((f32[512,512]{1,0:T(8,128)}), f32[8192,512]{1,0:T(8,128)}) %all-gather.30.cloned.1.call-update) | async-done | bytes 16777232 | tf_op jit(solution)/shard_map/all_gather | solution.py:14
  792.4 39.3 %custom-call.30 = f32[4,128,128]{1,2,0:T(8,128)S(1)} custom-call(f32[4,128,128]{2,1,0:T(8,128)S(1)} %get-tuple-element.19), custom_call_target="InvertDiagBlocksLowerTriangular" | custom-call | tf_op jit(solution)/shard_map/triangular_solve/custom-call.3 | solution.py:120
  845.7 85.5 %all-gather.32.cloned.1.call-done = f32[8192,512]{0,1:T(8,128)} async-done(((f32[1024,512]{0,1:T(8,128)}), f32[8192,512]{0,1:T(8,128)}) %all-gather.32.cloned.1.call-update) | async-done | bytes 16777232 | tf_op jit(solution)/shard_map/all_gather | solution.py:14
  931.2 19.9 copy.36
  959.8 196.1 %all-gather.36.cloned.1.call-done = f32[16384,512]{0,1:T(8,128)} async-done(((f32[1024,512]{0,1:T(8,128)}), f32[16384,512]{0,1:T(8,128)}) %all-gather.36.cloned.1.call-update) | async-done | bytes 33554448 | tf_op jit(solution)/shard_map/all_gather | solution.py:14
  1155.9 32.9 %copy.38 = f32[64,8,16,1024]{3,2,1,0:T(8,128)S(1)} copy(f32[64,8,16,1024]{3,1,2,0:T(8,128)} %bitcast.169) | data formatting | bytes 67108864
  1198.5 156.7 %all-gather.34.cloned.1.call-done = f32[16384,512]{0,1:T(8,128)} async-done(((f32[1024,512]{0,1:T(8,128)}), f32[16384,512]{0,1:T(8,128)}) %all-gather.34.cloned.1.call-update) | async-done | bytes 33554448 | tf_op jit(solution)/shard_map/all_gather | solution.py:14
  1355.2 32.5 %copy.37 = f32[64,8,16,1024]{3,2,1,0:T(8,128)S(1)} copy(f32[64,8,16,1024]{3,1,2,0:T(8,128)} %bitcast.171) | data formatting | bytes 67108864
  1419.1 110.6 %all-gather.38.cloned.1.call-done = f32[8192,512]{1,0:T(8,128)} async-done(((f32[512,512]{1,0:T(8,128)}), f32[8192,512]{1,0:T(8,128)}) %all-gather.38.cloned.1.call-update) | async-done | bytes 16777232 | tf_op jit(solution)/shard_map/all_gather | solution.py:14
  1642.1 39.3 %custom-call.34 = f32[4,128,128]{1,2,0:T(8,128)S(1)} custom-call(f32[4,128,128]{2,1,0:T(8,128)S(1)} %get-tuple-element.20), custom_call_target="InvertDiagBlocksLowerTriangular" | custom-call | tf_op jit(solution)/shard_map/triangular_solve/custom-call.3 | solution.py:120
  1695.6 85.5 %all-gather.40.cloned.1.call-done = f32[8192,512]{0,1:T(8,128)} async-done(((f32[1024,512]{0,1:T(8,128)}), f32[8192,512]{0,1:T(8,128)}) %all-gather.40.cloned.1.call-update) | async-done | bytes 16777232 | tf_op jit(solution)/shard_map/all_gather | solution.py:14
  1781.2 19.9 copy.39
  1819.6 186.4 %all-gather.44.cloned.1.call-done = f32[16384,512]{0,1:T(8,128)} async-done(((f32[1024,512]{0,1:T(8,128)}), f32[16384,512]{0,1:T(8,128)}) %all-gather.44.cloned.1.call-update) | async-done | bytes 33554448 | tf_op jit(solution)/shard_map/all_gather | solution.py:14
  2006.0 32.5 %copy.41 = f32[64,8,16,1024]{3,2,1,0:T(8,128)S(1)} copy(f32[64,8,16,1024]{3,1,2,0:T(8,128)} %bitcast.168) | data formatting | bytes 67108864
  2046.9 157.8 %all-gather.42.cloned.1.call-done = f32[16384,512]{0,1:T(8,128)} async-done(((f32[1024,512]{0,1:T(8,128)}), f32[16384,512]{0,1:T(8,128)}) %all-gather.42.cloned.1.call-update) | async-done | bytes 33554448 | tf_op jit(solution)/shard_map/all_gather | solution.py:14
  2204.8 32.5 %copy.40 = f32[64,8,16,1024]{3,2,1,0:T(8,128)S(1)} copy(f32[64,8,16,1024]{3,1,2,0:T(8,128)} %bitcast.170) | data formatting | bytes 67108864
  2247.0 17.6 fusion.12
  (202 shorter events, 422.3 us)
Async XLA Ops:
  7.2 97.9 %copy-start = (bf16[128,4096]{1,0:T(8,128)(2,1)S(1)}, bf16[128,4096]{1,0:T(8,128)(2,1)}, u32[]{:S(2)}) copy-start(bf16[128,4096]{1,0:T(8,128)(2,1)} %param.10) | copy-start | bytes 3145732
  113.1 17.7 all-to-all-start
  119.8 35.2 %all-gather.24.cloned.1.call-start = ((), (), s32[]{:S(2)}) async-start(), calls=%async_computation.1 | async-start | bytes 2359296 | tf_op jit(solution)/shard_map/all_gather | solution.py:78
  132.7 222.9 %all-gather.26.cloned.1.call-start = ((), (), s32[]{:S(2)}) async-start(), calls=%async_computation.2 | async-start | bytes 35651584 | tf_op jit(solution)/shard_map/all_gather | solution.py:14
  158.9 61.2 %copy-start.9 = (s32[128]{0:T(128)S(1)}, s32[128]{0:T(128)}, u32[]{:S(2)}) copy-start(s32[128]{0:T(128)} %param.13) | copy-start | bytes 1540
  158.9 396.0 %all-gather.28.cloned.1.call-start = ((), (), s32[]{:S(2)}) async-start(), calls=%async_computation.3 | async-start | bytes 35651584 | tf_op jit(solution)/shard_map/all_gather | solution.py:14
  159.6 531.3 %all-gather.30.cloned.1.call-start = ((), (), s32[]{:S(2)}) async-start(), calls=%async_computation.4 | async-start | bytes 17825792 | tf_op jit(solution)/shard_map/all_gather | solution.py:14
  252.5 6.2 copy-start.8
  575.6 3.4 copy-start.5
  580.1 351.2 %all-gather.32.cloned.1.call-start = ((), (), s32[]{:S(2)}) async-start(), calls=%async_computation.5 | async-start | bytes 18874368 | tf_op jit(solution)/shard_map/all_gather | solution.py:14
  845.7 310.2 %all-gather.36.cloned.1.call-start = ((), (), s32[]{:S(2)}) async-start(), calls=%async_computation.7 | async-start | bytes 35651584 | tf_op jit(solution)/shard_map/all_gather | solution.py:14
  959.0 396.2 %all-gather.34.cloned.1.call-start = ((), (), s32[]{:S(2)}) async-start(), calls=%async_computation.6 | async-start | bytes 35651584 | tf_op jit(solution)/shard_map/all_gather | solution.py:14
  959.8 569.9 %all-gather.38.cloned.1.call-start = ((), (), s32[]{:S(2)}) async-start(), calls=%async_computation.8 | async-start | bytes 17825792 | tf_op jit(solution)/shard_map/all_gather | solution.py:14
  1387.7 9.7 copy-start.6
  1414.3 3.4 copy-start.2
  1418.8 362.4 %all-gather.40.cloned.1.call-start = ((), (), s32[]{:S(2)}) async-start(), calls=%async_computation.9 | async-start | bytes 18874368 | tf_op jit(solution)/shard_map/all_gather | solution.py:14
  1540.4 1.0 copy-start.7
  1695.6 310.4 %all-gather.44.cloned.1.call-start = ((), (), s32[]{:S(2)}) async-start(), calls=%async_computation.11 | async-start | bytes 35651584 | tf_op jit(solution)/shard_map/all_gather | solution.py:14
  1806.4 2.7 copy-start.3
  1809.2 395.6 %all-gather.42.cloned.1.call-start = ((), (), s32[]{:S(2)}) async-start(), calls=%async_computation.10 | async-start | bytes 35651584 | tf_op jit(solution)/shard_map/all_gather | solution.py:14
  2237.3 9.7 copy-start.4
  2247.0 17.6 copy-start.1
Sparse Core Ops, SparseCore 0:
  132.8 22.1 all-gather.23
  159.0 196.5 all-gather.25
  358.4 196.4 all-gather.27
  580.2 110.7 all-gather.29
  845.8 85.3 all-gather.31
  959.2 196.6 all-gather.35
  1158.6 196.5 all-gather.33
  1418.9 110.7 all-gather.37
  1695.7 85.3 all-gather.39
  1809.3 196.6 all-gather.43
  2008.2 196.5 all-gather.41
